TPU v7x, 256 devices: a whole 4x4x8 slice. The times are simulated.
256 devices in a mesh: dp: 16 (over x, y), head: 16 (over z, core).
Axes of the slice: x: 4, y: 4, z: 8, core: 2. Of those that a mesh axis runs over, the one named last changes fastest.
Arguments:
- latents: bfloat16 [2048, 512], P('dp'), may hold values from -6 to 6
- targets: bfloat16 [2048, 32768], P('dp', 'head'), may hold values from -6 to 6
- kv_weight: bfloat16 [512, 32768], P(None, 'head'), may hold values from -0.25 to 0.25
- momentum: float32 [512, 16, 2048], P(None, 'head', 'dp'), may hold values from -120 to 120
Outputs:
- momentum_out: float32 [512, 16, 2048], P(None, 'head', 'dp')
- update: float32 [512, 16, 2048], P(None, 'head', 'dp')
All inputs are finite; a program needn't handle non-finite values.
Results may differ from a plain program's by a relative error of at most 0.0003.
The roundings to bfloat16 on the way count: a program that leaves them out, or rounds other values in their place, can miss the bound.
Values may be sent and summed in bfloat16 or wider, within the bound.
A program may use at most 64 MiB of HBM per device.

v0:
```python
import math
import jax
import jax.numpy as jnp
from jax import lax
from jax.sharding import PartitionSpec as P

C = 32768
ITERS = 2
decay_rate = 0.95
linear_coef = 3.4445
square_coef = -4.775
quint_coef = 2.0315
epsilon = 1e-07


def gram_total(iterate):
    local_gram = lax.dot_general(
        iterate, iterate, (((1,), (1,)), ((), ())), precision=lax.Precision.HIGHEST
    )
    return lax.psum(local_gram, ("dp", "head"))


def local(latents, targets, kv_weight, momentum):
    latent_width = momentum.shape[0]
    sub_width = momentum.shape[2]
    total_tokens = latents.shape[0] * lax.axis_size("dp")
    residual = (
        jnp.dot(latents, kv_weight, preferred_element_type=jnp.float32)
        - targets.astype(jnp.float32)
    ).astype(jnp.bfloat16)
    gradient = lax.psum_scatter(
        lax.dot_general(
            residual, latents, (((0,), (0,)), ((), ())), preferred_element_type=jnp.float32
        ),
        "dp",
        scatter_dimension=0,
        tiled=True,
    ).T
    gradient = gradient * (1.0 / math.sqrt(total_tokens))
    previous = momentum.reshape(latent_width, sub_width)
    momentum_new = decay_rate * previous + gradient
    nesterov = gradient + decay_rate * momentum_new
    squares = lax.psum(jnp.sum(nesterov * nesterov), ("dp", "head"))
    inverse = 1.0 / (jnp.sqrt(squares) + epsilon)
    iterate = nesterov * inverse
    gram_matrix = gram_total(iterate)
    for iteration in range(ITERS):
        if iteration > 0:
            gram_matrix = gram_total(iterate)
        polynomial = square_coef * gram_matrix + quint_coef * jnp.dot(
            gram_matrix, gram_matrix, precision=lax.Precision.HIGHEST
        )
        iterate = linear_coef * iterate + jnp.dot(
            polynomial, iterate, precision=lax.Precision.HIGHEST
        )
    update = iterate * math.sqrt(C)
    return (
        momentum_new.reshape(latent_width, 1, sub_width),
        update.reshape(latent_width, 1, sub_width),
    )


def solution(mesh):
    return jax.shard_map(
        local,
        mesh=mesh,
        in_specs=(P("dp", None), P("dp", "head"), P(None, "head"), P(None, "head", "dp")),
        out_specs=(P(None, "head", "dp"), P(None, "head", "dp")),
        check_vma=False,
    )
```

profile of v0, /device:TPU:2, one launch (start us, length us, event | category | flops | bytes accessed | tf_op | source)
XLA Modules:
  0.0 706.9 jit_solution(13692104984853528014)
XLA Ops:
  7.2 0.0 copy-start
  7.2 0.0 reduce-scatter.2.cloned.1.call-start
  7.2 1.5 copy-done
  8.8 4.0 fusion.3
  12.8 0.0 copy-start.2
  12.8 0.0 reduce-scatter.2.cloned.1.call-update
  12.8 0.0 all-reduce.3.cloned.1.call-start
  12.9 0.9 copy-done.2
  13.7 0.1 copy.6
  13.9 84.5 %reduce-scatter.2.cloned.1.call-done = f32[128,512]{1,0:T(8,128)} async-done(((f32[2048,512]{1,0:T(8,128)}), f32[128,512]{1,0:T(8,128)}) %reduce-scatter.2.cloned.1.call-update) | async-done | bytes 262160 | tf_op jit(solution)/shard_map/reduce_scatter | solution.py:31
  98.3 1.6 multiply_reduce_fusion
  99.9 73.7 %psum.21 = f32[]{:T(128)} all-reduce(f32[]{:T(128)} %get-tuple-element.4), channel_id=1, replica_groups=mesh['dp'=16,'head'=16] {'dp','head'}, use_global_device_ids=true, to_apply=%region_2.0 | all-reduce | flops 1 | bytes 8 | tf_op jit(solution)/shard_map/psum | solution.py:43
  174.3 3.1 fusion.7
  177.5 0.0 copy-start.1
  177.5 0.0 all-reduce.3.cloned.1.call-update
  177.5 0.0 all-reduce.5.cloned.1.call-start
  177.5 254.9 %all-reduce.3.cloned.1.call-done = f32[512,512]{1,0:T(8,128)} async-done(((f32[512,512]{1,0:T(8,128)}), f32[512,512]{1,0:T(8,128)}) %all-reduce.3.cloned.1.call-update) | async-done | bytes 1048592 | tf_op jit(solution)/shard_map/psum | solution.py:20
  432.5 3.9 fusion.2
  436.4 0.0 copy-done.1
  436.4 1.2 convolution_add_fusion.1
  437.6 2.1 fusion.13
  439.7 0.0 all-reduce.5.cloned.1.call-update
  439.7 0.8 copy.9
  440.6 253.9 %all-reduce.5.cloned.1.call-done = f32[512,512]{1,0:T(8,128)} async-done(((f32[512,512]{1,0:T(8,128)}), f32[512,512]{1,0:T(8,128)}) %all-reduce.5.cloned.1.call-update) | async-done | bytes 1048592 | tf_op jit(solution)/shard_map/psum | solution.py:20
  694.4 3.9 fusion.1
  698.3 1.2 fusion.5
  699.6 0.8 copy.10
Async XLA Ops:
  7.2 1.6 copy-start
  7.2 91.1 %reduce-scatter.2.cloned.1.call-start = ((), (), s32[]{:S(2)}) async-start(), calls=%async_computation.1 | async-start | bytes 4456448 | tf_op jit(solution)/shard_map/reduce_scatter | solution.py:31
  12.8 0.9 copy-start.2
  12.8 419.7 %all-reduce.3.cloned.1.call-start = ((), (), s32[]{:S(2)}) async-start(), calls=%async_computation.2 | async-start | bytes 2097152 | tf_op jit(solution)/shard_map/psum | solution.py:20
  177.5 258.9 %copy-start.1 = (f32[128,512]{1,0:T(8,128)S(1)}, f32[128,512]{1,0:T(8,128)}, u32[]{:S(2)}) copy-start(f32[128,512]{1,0:T(8,128)} %reduce-scatter.2.cloned.1.call-done) | copy-start | bytes 786436
  177.5 516.9 %all-reduce.5.cloned.1.call-start = ((), (), s32[]{:S(2)}) async-start(), calls=%async_computation.3 | async-start | bytes 2097152 | tf_op jit(solution)/shard_map/psum | solution.py:20
Sparse Core Ops, SparseCore 0:
  12.9 85.3 reduce-scatter.1
  177.6 254.8 all-reduce.2
  439.9 254.5 all-reduce.4
where the time goes:
time: 707 us
  waiting for transfers between devices  593 us (84%)
  blocking collectives  73.7 us (10%)
  matrix products  19.5 us (3%)
  between operations  14.5 us (2%)
    psum x2, waiting for transfers between devices, gram_total(): return lax.psum(local_gram, ('dp', 'head'))  509 us
    reduce_scatter x1, waiting for transfers between devices, local(): lax.psum_scatter(lax.dot_general(residual, latents, (((0,), (0,)), ((), (...  84.5 us
    psum x1, blocking collectives, local(): squares = lax.psum(jnp.sum(nesterov * nesterov), ('dp', 'head'))  73.7 us
  transfers between devices with their start and end apart: 3, of which 3 were waited for; matrix products, arithmetic and copies ran while one was open for 0% of the time, Pallas kernels for 0%

commit v1 on v0

--- a/solution.py
+++ b/solution.py
@@ -17,7 +17,7 @@
     local_gram = lax.dot_general(
         iterate, iterate, (((1,), (1,)), ((), ())), precision=lax.Precision.HIGHEST
     )
-    return lax.psum(local_gram, ("dp", "head"))
+    return lax.psum(lax.psum(local_gram, "head"), "dp")
 
 
 def local(latents, targets, kv_weight, momentum):

time: 707 us -> 620 us (0.88)
  waiting for transfers between devices: 593 us -> 506 us
    psum x2 -> x4, waiting for transfers between devices: 509 us -> 421 us  [gram_total(): return lax.psum(lax.psum(local_gram, 'head'), 'dp')]
  transfers between devices with their start and end apart: 3 -> 5, of which waited for: 3 -> 5; matrix products, arithmetic and copies ran while one was open for 0% -> 0% of each run, Pallas kernels for 0% -> 0%
where the time goes in v1:
time: 620 us
  waiting for transfers between devices  506 us (82%)
  blocking collectives  73.7 us (12%)
  matrix products  19.9 us (3%)
  between operations  14.6 us (2%)
    psum x4, waiting for transfers between devices, gram_total(): return lax.psum(lax.psum(local_gram, 'head'), 'dp')  421 us
    reduce_scatter x1, waiting for transfers between devices, local(): lax.psum_scatter(lax.dot_general(residual, latents, (((0,), (0,)), ((), (...  84.5 us
    psum x1, blocking collectives, local(): squares = lax.psum(jnp.sum(nesterov * nesterov), ('dp', 'head'))  73.7 us
  transfers between devices with their start and end apart: 5, of which 5 were waited for; matrix products, arithmetic and copies ran while one was open for 0% of the time, Pallas kernels for 0%

profile of v1, /device:TPU:2, one launch (start us, length us, event | category | flops | bytes accessed | tf_op | source)
XLA Modules:
  0.0 619.9 jit_solution(1630520352334423915)
XLA Ops:
  7.2 0.0 copy-start
  7.2 0.0 reduce-scatter.2.cloned.1.call-start
  7.2 1.5 copy-done
  8.8 4.0 fusion.3
  12.8 0.0 copy-start.2
  12.8 0.0 reduce-scatter.2.cloned.1.call-update
  12.8 0.0 all-reduce.5.cloned.1.call-start
  12.9 0.9 copy-done.2
  13.7 0.1 copy.6
  13.9 84.5 %reduce-scatter.2.cloned.1.call-done = f32[128,512]{1,0:T(8,128)} async-done(((f32[2048,512]{1,0:T(8,128)}), f32[128,512]{1,0:T(8,128)}) %reduce-scatter.2.cloned.1.call-update) | async-done | bytes 262160 | tf_op jit(solution)/shard_map/reduce_scatter | solution.py:31
  98.3 1.6 multiply_reduce_fusion
  99.9 73.7 %psum.35 = f32[]{:T(128)} all-reduce(f32[]{:T(128)} %get-tuple-element.4), channel_id=1, replica_groups=mesh['dp'=16,'head'=16] {'dp','head'}, use_global_device_ids=true, to_apply=%region_2.0 | all-reduce | flops 1 | bytes 8 | tf_op jit(solution)/shard_map/psum | solution.py:43
  174.3 3.1 fusion.7
  177.5 0.0 all-reduce.5.cloned.1.call-update
  177.5 0.0 all-reduce.7.cloned.1.call-start
  177.5 110.3 %all-reduce.5.cloned.1.call-done = f32[512,512]{1,0:T(8,128)} async-done(((f32[512,512]{1,0:T(8,128)}), f32[512,512]{1,0:T(8,128)}) %all-reduce.5.cloned.1.call-update) | async-done | bytes 1048592 | tf_op jit(solution)/shard_map/psum | solution.py:20
  287.9 0.0 copy-start.1
  287.9 0.0 all-reduce.7.cloned.1.call-update
  287.9 0.0 all-reduce.9.cloned.1.call-start
  287.9 100.2 %all-reduce.7.cloned.1.call-done = f32[512,512]{1,0:T(8,128)} async-done(((f32[512,512]{1,0:T(8,128)}), f32[512,512]{1,0:T(8,128)}) %all-reduce.7.cloned.1.call-update) | async-done | bytes 1048592 | tf_op jit(solution)/shard_map/psum | solution.py:20
  388.1 4.1 fusion.2
  392.2 0.0 copy-done.1
  392.2 1.2 convolution_add_fusion.1
  393.5 2.1 fusion.13
  395.5 0.0 all-reduce.9.cloned.1.call-update
  395.6 0.0 all-reduce.11.cloned.1.call-start
  395.6 111.2 %all-reduce.9.cloned.1.call-done = f32[512,512]{1,0:T(8,128)} async-done(((f32[512,512]{1,0:T(8,128)}), f32[512,512]{1,0:T(8,128)}) %all-reduce.9.cloned.1.call-update) | async-done | bytes 1048592 | tf_op jit(solution)/shard_map/psum | solution.py:20
  506.8 0.0 all-reduce.11.cloned.1.call-update
  506.8 0.8 copy.9
  507.7 99.5 %all-reduce.11.cloned.1.call-done = f32[512,512]{1,0:T(8,128)} async-done(((f32[512,512]{1,0:T(8,128)}), f32[512,512]{1,0:T(8,128)}) %all-reduce.11.cloned.1.call-update) | async-done | bytes 1048592 | tf_op jit(solution)/shard_map/psum | solution.py:20
  607.2 4.1 fusion.1
  611.3 1.2 fusion.5
  612.5 0.8 copy.10
Async XLA Ops:
  7.2 1.6 copy-start
  7.2 91.1 %reduce-scatter.2.cloned.1.call-start = ((), (), s32[]{:S(2)}) async-start(), calls=%async_computation.1 | async-start | bytes 4456448 | tf_op jit(solution)/shard_map/reduce_scatter | solution.py:31
  12.8 0.9 copy-start.2
  12.8 275.1 %all-reduce.5.cloned.1.call-start = ((), (), s32[]{:S(2)}) async-start(), calls=%async_computation.2 | async-start | bytes 2097152 | tf_op jit(solution)/shard_map/psum | solution.py:20
  177.5 210.6 %all-reduce.7.cloned.1.call-start = ((), (), s32[]{:S(2)}) async-start(), calls=%async_computation.3 | async-start | bytes 2097152 | tf_op jit(solution)/shard_map/psum | solution.py:20
  287.9 104.4 %copy-start.1 = (f32[128,512]{1,0:T(8,128)S(1)}, f32[128,512]{1,0:T(8,128)}, u32[]{:S(2)}) copy-start(f32[128,512]{1,0:T(8,128)} %reduce-scatter.2.cloned.1.call-done) | copy-start | bytes 786436
  287.9 218.9 %all-reduce.9.cloned.1.call-start = ((), (), s32[]{:S(2)}) async-start(), calls=%async_computation.4 | async-start | bytes 2097152 | tf_op jit(solution)/shard_map/psum | solution.py:20
  395.6 211.6 %all-reduce.11.cloned.1.call-start = ((), (), s32[]{:S(2)}) async-start(), calls=%async_computation.5 | async-start | bytes 2097152 | tf_op jit(solution)/shard_map/psum | solution.py:20
Sparse Core Ops, SparseCore 0:
  12.9 85.3 reduce-scatter.1
  177.6 110.2 all-reduce.4
  291.1 96.9 all-reduce.6
  395.7 111.0 all-reduce.8
  510.2 96.9 all-reduce.10
